TPU v7x, 32 devices: a whole 2x2x4 slice. The times are simulated.
32 devices in a mesh: fsdp: 4 (over z), replica: 2 (over x), ctx: 4 (over y, core).
Axes of the slice: x: 2, y: 2, z: 4, core: 2. Of those that a mesh axis runs over, the one named last changes fastest.
Arguments:
- hidden_in: bfloat16 [8, 1088, 2048], P(('fsdp', 'replica'), 'ctx'), may hold values from -6 to 6
- memory_rows: bfloat16 [8, 50, 2048], P(('fsdp', 'replica')), may hold values from -6 to 6
- seg_len: int32 [8], P(('fsdp', 'replica')), may hold values from 519 to 1038, as said below
- out_grad: bfloat16 [8, 1088, 2048], P(('fsdp', 'replica'), 'ctx'), may hold values from -6 to 6
- first_gain: bfloat16 [2048], P('fsdp'), may hold values from 0.5 to 1.5
- first_shift: bfloat16 [2048], P('fsdp'), may hold values from -1 to 1
- qkv_weight: bfloat16 [2048, 6144], P('fsdp'), may hold values from -0.125 to 0.125
- query_bias: bfloat16 [2048], P('fsdp'), may hold values from -4 to 4
- value_bias: bfloat16 [2048], P('fsdp'), may hold values from -2.5 to 2.5
- out_weight: bfloat16 [2048, 2048], P('fsdp'), may hold values from -2 to 2
- out_bias: bfloat16 [2048], P('fsdp'), may hold values from -1 to 1
- second_gain: bfloat16 [2048], P('fsdp'), may hold values from 0.5 to 1.5
- second_shift: bfloat16 [2048], P('fsdp'), may hold values from -1 to 1
- up_weight: bfloat16 [2048, 8192], P('fsdp'), may hold values from -0.125 to 0.125
- up_bias: bfloat16 [8192], P('fsdp'), may hold values from -1 to 1
- down_weight: bfloat16 [8192, 2048], P('fsdp'), may hold values from -0.0625 to 0.0625
- down_bias: bfloat16 [2048], P('fsdp'), may hold values from -1 to 1
Outputs:
- output: bfloat16 [8, 1088, 2048], P(('fsdp', 'replica'), 'ctx')
- input_grad: float32 [8, 1088, 2048], P(('fsdp', 'replica'), 'ctx')
- memory_grad: float32 [8, 50, 2048], P(('fsdp', 'replica'))
- first_gain_grad: float32 [2048], P('fsdp')
- first_shift_grad: float32 [2048], P('fsdp')
- qkv_weight_grad: float32 [2048, 6144], P('fsdp')
- query_bias_grad: float32 [2048], P('fsdp')
- value_bias_grad: float32 [2048], P('fsdp')
- out_weight_grad: float32 [2048, 2048], P('fsdp')
- out_bias_grad: float32 [2048], P('fsdp')
- second_gain_grad: float32 [2048], P('fsdp')
- second_shift_grad: float32 [2048], P('fsdp')
- up_weight_grad: float32 [2048, 8192], P('fsdp')
- up_bias_grad: float32 [8192], P('fsdp')
- down_weight_grad: float32 [8192, 2048], P('fsdp')
- down_bias_grad: float32 [2048], P('fsdp')
Inputs may be any that keep to these rules, and one draw needn't show every extreme that they name: Positions seg_len to 1037 of a segment are padding that no query uses as a key.
All inputs are finite; a program needn't handle non-finite values.
Results may differ from a plain program's by a relative error of at most 0.015.
Values may be sent and summed in bfloat16 or wider, within the bound.
No kernel may reach another device: no remote copies, remote signals or barrier semaphores. Data moves between devices by JAX's collectives and lax.ppermute only.
A program may use at most 512 MiB of HBM per device.

v0:
```python
import jax
import jax.numpy as jnp
from jax import lax
from jax.sharding import PartitionSpec as P

D = 2048
HEADS = 32
HEAD_DIM = 64
SUMM = 50
SEQ_LEN = 1088
SEG = 1038
epsilon = 1e-05
masked = -1e30


def smooth_unit(values):
    return jax.nn.gelu(values, approximate=False)


def layer_norm(inputs, weight, offset):
    average = jnp.mean(inputs, axis=-1, keepdims=True)
    centred = inputs - average
    spread = jnp.mean(centred * centred, axis=-1, keepdims=True)
    inverse = lax.rsqrt(spread + epsilon)
    normal = centred * inverse
    return (normal * weight + offset, normal, inverse)


def norm_back(upstream, normal, inverse, weight):
    scaled = upstream * weight
    centre_term = jnp.mean(scaled, axis=-1, keepdims=True)
    slope_term = jnp.mean(scaled * normal, axis=-1, keepdims=True)
    return (
        inverse * (scaled - centre_term - normal * slope_term),
        jnp.sum(upstream * normal, axis=0),
        jnp.sum(upstream, axis=0),
    )


def across(left, right):
    return lax.dot_general(
        left, right, (((0,), (0,)), ((), ())), preferred_element_type=jnp.float32
    )


def against(left, right):
    return lax.dot_general(
        left, right, (((1,), (1,)), ((), ())), preferred_element_type=jnp.float32
    )


def head_slice(array, block_index, block_width, head_group):
    piece = lax.dynamic_slice_in_dim(array, block_index * block_width, block_width, 2)
    return piece.reshape(piece.shape[0], piece.shape[1], head_group, block_width // head_group)


def shards(
    hidden_in,
    memory_rows,
    seg_len,
    out_grad,
    first_gain,
    first_shift,
    qkv_weight,
    query_bias,
    value_bias,
    out_weight,
    out_bias,
    second_gain,
    second_shift,
    up_weight,
    up_bias,
    down_weight,
    down_bias,
):
    gathered = (
        lax.all_gather(first_gain, "fsdp", axis=0, tiled=True),
        lax.all_gather(first_shift, "fsdp", axis=0, tiled=True),
        lax.all_gather(qkv_weight, "fsdp", axis=0, tiled=True),
        lax.all_gather(query_bias, "fsdp", axis=0, tiled=True),
        lax.all_gather(value_bias, "fsdp", axis=0, tiled=True),
        lax.all_gather(out_weight, "fsdp", axis=0, tiled=True),
        lax.all_gather(out_bias, "fsdp", axis=0, tiled=True),
        lax.all_gather(second_gain, "fsdp", axis=0, tiled=True),
        lax.all_gather(second_shift, "fsdp", axis=0, tiled=True),
        lax.all_gather(up_weight, "fsdp", axis=0, tiled=True),
        lax.all_gather(up_bias, "fsdp", axis=0, tiled=True),
        lax.all_gather(down_weight, "fsdp", axis=0, tiled=True),
        lax.all_gather(down_bias, "fsdp", axis=0, tiled=True),
    )
    gain_one = gathered[0].astype(jnp.float32)
    shift_one = gathered[1].astype(jnp.float32)
    bias_query = gathered[3].astype(jnp.float32)
    bias_value = gathered[4].astype(jnp.float32)
    bias_out = gathered[6].astype(jnp.float32)
    gain_two = gathered[7].astype(jnp.float32)
    shift_two = gathered[8].astype(jnp.float32)
    bias_up = gathered[10].astype(jnp.float32)
    bias_down = gathered[12].astype(jnp.float32)
    weight_qkv = gathered[2]
    weight_out = gathered[5]
    weight_up = gathered[9]
    weight_down = gathered[11]
    groups = hidden_in.shape[0]
    span_rows = hidden_in.shape[1]
    row_count = groups * span_rows
    mem_count = groups * SUMM
    key_count = SUMM + SEQ_LEN
    head_group = min(8, HEADS)
    group_count = HEADS // head_group
    block_width = head_group * HEAD_DIM
    tokens = hidden_in.reshape(row_count, D).astype(jnp.float32)
    normed, normal_one, inverse_one = layer_norm(tokens, gain_one, shift_one)
    normed_low = normed.astype(jnp.bfloat16)
    memory = memory_rows.reshape(mem_count, D).astype(jnp.float32)
    mem_normed, mem_normal, mem_inverse = layer_norm(memory, gain_one, shift_one)
    mem_low = mem_normed.astype(jnp.bfloat16)
    projected = jnp.dot(normed_low, weight_qkv, preferred_element_type=jnp.float32)
    mem_projected = jnp.dot(mem_low, weight_qkv[:, D:], preferred_element_type=jnp.float32)
    query = (
        ((projected[:, :D] + bias_query) * 0.125).astype(jnp.bfloat16).reshape(groups, span_rows, D)
    )
    keys_local = projected[:, D : 2 * D].astype(jnp.bfloat16).reshape(groups, span_rows, D)
    values_local = (
        (projected[:, 2 * D :] + bias_value).astype(jnp.bfloat16).reshape(groups, span_rows, D)
    )
    mem_keys = mem_projected[:, :D].astype(jnp.bfloat16).reshape(groups, SUMM, D)
    mem_values = (mem_projected[:, D:] + bias_value).astype(jnp.bfloat16).reshape(groups, SUMM, D)
    keys_seq, values_seq = (
        lax.all_gather(keys_local, "ctx", axis=1, tiled=True),
        lax.all_gather(values_local, "ctx", axis=1, tiled=True),
    )
    keys_all = jnp.concatenate([mem_keys, keys_seq], axis=1)
    values_all = jnp.concatenate([mem_values, values_seq], axis=1)
    positions = lax.axis_index("ctx") * span_rows + jnp.arange(span_rows, dtype=jnp.int32)
    key_places = jnp.arange(SEQ_LEN, dtype=jnp.int32)
    causal = key_places[None, :] <= positions[:, None]
    present = (key_places[None, :] < seg_len[:, None]) | (key_places[None, :] >= SEG)
    allowed = jnp.concatenate(
        [jnp.ones((groups, span_rows, SUMM), dtype=bool), causal[None] & present[:, None, :]],
        axis=2,
    )[:, None]

    def attend(block_index):
        query_block = head_slice(query, block_index, block_width, head_group)
        key_block = head_slice(keys_all, block_index, block_width, head_group)
        value_block = head_slice(values_all, block_index, block_width, head_group)
        scores = jnp.einsum(
            "gqhd,gkhd->ghqk", query_block, key_block, preferred_element_type=jnp.float32
        )
        scores = jnp.where(allowed, scores, masked)
        largest = jnp.max(scores, axis=-1, keepdims=True)
        expanded = jnp.exp(scores - largest)
        totals = jnp.sum(expanded, axis=-1, keepdims=True)
        weights_low = (expanded / totals).astype(jnp.bfloat16)
        mixed_rows = jnp.einsum(
            "ghqk,gkhd->gqhd", weights_low, value_block, preferred_element_type=jnp.float32
        )
        return (mixed_rows.reshape(groups, span_rows, block_width), largest + jnp.log(totals))

    mixed_blocks, log_totals = lax.map(attend, jnp.arange(group_count))
    attended = jnp.moveaxis(mixed_blocks, 0, 2).reshape(row_count, D).astype(jnp.bfloat16)
    branch = jnp.dot(attended, weight_out, preferred_element_type=jnp.float32) + bias_out
    middle = tokens + branch
    normed_two, normal_two, inverse_two = layer_norm(middle, gain_two, shift_two)
    normed_two_low = normed_two.astype(jnp.bfloat16)
    upper = jnp.dot(normed_two_low, weight_up, preferred_element_type=jnp.float32) + bias_up
    active_float, smooth_pull = jax.vjp(smooth_unit, upper)
    active = active_float.astype(jnp.bfloat16)
    output = (
        (middle + (jnp.dot(active, weight_down, preferred_element_type=jnp.float32) + bias_down))
        .astype(jnp.bfloat16)
        .reshape(groups, span_rows, D)
    )
    again = (
        lax.all_gather(qkv_weight, "fsdp", axis=0, tiled=True),
        lax.all_gather(out_weight, "fsdp", axis=0, tiled=True),
        lax.all_gather(up_weight, "fsdp", axis=0, tiled=True),
        lax.all_gather(down_weight, "fsdp", axis=0, tiled=True),
    )
    back_qkv = again[0]
    back_out = again[1]
    back_up = again[2]
    back_down = again[3]
    cotangent = out_grad.reshape(row_count, D)
    cot_float = cotangent.astype(jnp.float32)
    down_part = lax.psum_scatter(
        across(active, cotangent).astype(jnp.bfloat16), "fsdp", scatter_dimension=0, tiled=True
    ).astype(jnp.float32)
    hidden_grad = against(cotangent, back_down)
    upper_grad = smooth_pull(hidden_grad)[0].astype(jnp.bfloat16)
    up_part = lax.psum_scatter(
        across(normed_two_low, upper_grad).astype(jnp.bfloat16),
        "fsdp",
        scatter_dimension=0,
        tiled=True,
    ).astype(jnp.float32)
    normed_two_grad = against(upper_grad, back_up)
    middle_norm_grad, gain_two_grad, shift_two_grad = norm_back(
        normed_two_grad, normal_two, inverse_two, gain_two
    )
    middle_grad = cot_float + middle_norm_grad
    branch_grad = middle_grad.astype(jnp.bfloat16)
    out_weight_grad = across(attended, branch_grad)
    mixed_grad = against(branch_grad, back_out).astype(jnp.bfloat16).reshape(groups, span_rows, D)

    def attend_back(block_index):
        query_block = head_slice(query, block_index, block_width, head_group)
        key_block = head_slice(keys_all, block_index, block_width, head_group)
        value_block = head_slice(values_all, block_index, block_width, head_group)
        grad_block = head_slice(mixed_grad, block_index, block_width, head_group)
        scores = jnp.einsum(
            "gqhd,gkhd->ghqk", query_block, key_block, preferred_element_type=jnp.float32
        )
        scores = jnp.where(allowed, scores, masked)
        weights = jnp.exp(scores - log_totals[block_index])
        value_grad = jnp.einsum(
            "ghqk,gqhd->gkhd",
            weights.astype(jnp.bfloat16),
            grad_block,
            preferred_element_type=jnp.float32,
        )
        weight_grad = jnp.einsum(
            "gqhd,gkhd->ghqk", grad_block, value_block, preferred_element_type=jnp.float32
        )
        centre = jnp.sum(weights * weight_grad, axis=-1, keepdims=True)
        score_grad = (weights * (weight_grad - centre)).astype(jnp.bfloat16)
        query_grad = jnp.einsum(
            "ghqk,gkhd->gqhd", score_grad, key_block, preferred_element_type=jnp.float32
        )
        key_grad = jnp.einsum(
            "ghqk,gqhd->gkhd", score_grad, query_block, preferred_element_type=jnp.float32
        )
        return (
            query_grad.reshape(groups, span_rows, block_width),
            key_grad.reshape(groups, key_count, block_width),
            value_grad.reshape(groups, key_count, block_width),
        )

    query_blocks, key_blocks, value_blocks = lax.map(attend_back, jnp.arange(group_count))
    query_grad_all = jnp.moveaxis(query_blocks, 0, 2).reshape(groups, span_rows, D)
    key_grad_all = jnp.moveaxis(key_blocks, 0, 2).reshape(groups, key_count, D)
    value_grad_all = jnp.moveaxis(value_blocks, 0, 2).reshape(groups, key_count, D)
    key_sums, value_sums = (
        lax.psum_scatter(key_grad_all[:, SUMM:], "ctx", scatter_dimension=1, tiled=True),
        lax.psum_scatter(value_grad_all[:, SUMM:], "ctx", scatter_dimension=1, tiled=True),
    )
    mem_key_sums, mem_value_sums = lax.psum(
        (key_grad_all[:, :SUMM], value_grad_all[:, :SUMM]), "ctx"
    )
    qkv_grad = jnp.concatenate(
        [
            query_grad_all.astype(jnp.bfloat16) * 0.125,
            key_sums.astype(jnp.bfloat16),
            value_sums.astype(jnp.bfloat16),
        ],
        axis=2,
    ).reshape(row_count, 3 * D)
    mem_kv_grad = jnp.concatenate(
        [mem_key_sums.astype(jnp.bfloat16), mem_value_sums.astype(jnp.bfloat16)], axis=2
    ).reshape(mem_count, 2 * D)
    owner_flag = lax.axis_index("ctx") == 0
    first_owner = owner_flag.astype(jnp.float32)
    owned_mem_grad = jnp.where(owner_flag, mem_kv_grad, jnp.zeros_like(mem_kv_grad))
    mem_rows_grad = jnp.concatenate(
        [jnp.zeros((mem_count, D), jnp.bfloat16), owned_mem_grad], axis=1
    )
    qkv_weight_grad = across(
        jnp.concatenate([normed_low, mem_low], axis=0),
        jnp.concatenate([qkv_grad, mem_rows_grad], axis=0),
    )
    query_bias_grad = jnp.sum(qkv_grad[:, :D].astype(jnp.float32), axis=0)
    value_bias_grad = jnp.sum(qkv_grad[:, 2 * D :].astype(jnp.float32), axis=0) + jnp.sum(
        owned_mem_grad[:, D:].astype(jnp.float32), axis=0
    )
    out_bias_grad = jnp.sum(branch_grad.astype(jnp.float32), axis=0)
    up_bias_grad = jnp.sum(upper_grad.astype(jnp.float32), axis=0)
    down_bias_grad = jnp.sum(cot_float, axis=0)
    normed_grad = against(qkv_grad, back_qkv)
    token_norm_grad, gain_one_tok, shift_one_tok = norm_back(
        normed_grad, normal_one, inverse_one, gain_one
    )
    mem_normed_grad = against(mem_kv_grad, back_qkv[:, D:])
    memory_norm_grad, gain_one_mem, shift_one_mem = norm_back(
        mem_normed_grad, mem_normal, mem_inverse, gain_one
    )
    gain_one_grad = gain_one_tok + first_owner * gain_one_mem
    shift_one_grad = shift_one_tok + first_owner * shift_one_mem
    input_grad = (middle_grad + token_norm_grad).reshape(groups, span_rows, D)
    memory_grad = memory_norm_grad.reshape(groups, SUMM, D)
    shares = (
        lax.psum_scatter(
            gain_one_grad.astype(jnp.bfloat16), "fsdp", scatter_dimension=0, tiled=True
        ).astype(jnp.float32),
        lax.psum_scatter(
            shift_one_grad.astype(jnp.bfloat16), "fsdp", scatter_dimension=0, tiled=True
        ).astype(jnp.float32),
        lax.psum_scatter(
            qkv_weight_grad.astype(jnp.bfloat16), "fsdp", scatter_dimension=0, tiled=True
        ).astype(jnp.float32),
        lax.psum_scatter(
            query_bias_grad.astype(jnp.bfloat16), "fsdp", scatter_dimension=0, tiled=True
        ).astype(jnp.float32),
        lax.psum_scatter(
            value_bias_grad.astype(jnp.bfloat16), "fsdp", scatter_dimension=0, tiled=True
        ).astype(jnp.float32),
        lax.psum_scatter(
            out_weight_grad.astype(jnp.bfloat16), "fsdp", scatter_dimension=0, tiled=True
        ).astype(jnp.float32),
        lax.psum_scatter(
            out_bias_grad.astype(jnp.bfloat16), "fsdp", scatter_dimension=0, tiled=True
        ).astype(jnp.float32),
        lax.psum_scatter(
            gain_two_grad.astype(jnp.bfloat16), "fsdp", scatter_dimension=0, tiled=True
        ).astype(jnp.float32),
        lax.psum_scatter(
            shift_two_grad.astype(jnp.bfloat16), "fsdp", scatter_dimension=0, tiled=True
        ).astype(jnp.float32),
        lax.psum_scatter(
            up_bias_grad.astype(jnp.bfloat16), "fsdp", scatter_dimension=0, tiled=True
        ).astype(jnp.float32),
        lax.psum_scatter(
            down_bias_grad.astype(jnp.bfloat16), "fsdp", scatter_dimension=0, tiled=True
        ).astype(jnp.float32),
    )
    summed = lax.psum(
        (
            shares[0],
            shares[1],
            shares[2],
            shares[3],
            shares[4],
            shares[5],
            shares[6],
            shares[7],
            shares[8],
            shares[9],
            shares[10],
            up_part,
            down_part,
        ),
        ("replica", "ctx"),
    )
    return (
        output,
        input_grad,
        memory_grad,
        summed[0],
        summed[1],
        summed[2],
        summed[3],
        summed[4],
        summed[5],
        summed[6],
        summed[7],
        summed[8],
        summed[11],
        summed[9],
        summed[12],
        summed[10],
    )


def solution(mesh):
    return jax.shard_map(
        shards,
        mesh=mesh,
        in_specs=(
            P(("fsdp", "replica"), "ctx", None),
            P(("fsdp", "replica"), None, None),
            P(("fsdp", "replica")),
            P(("fsdp", "replica"), "ctx", None),
            P("fsdp"),
            P("fsdp"),
            P("fsdp", None),
            P("fsdp"),
            P("fsdp"),
            P("fsdp", None),
            P("fsdp"),
            P("fsdp"),
            P("fsdp"),
            P("fsdp", None),
            P("fsdp"),
            P("fsdp", None),
            P("fsdp"),
        ),
        out_specs=(
            P(("fsdp", "replica"), "ctx", None),
            P(("fsdp", "replica"), "ctx", None),
            P(("fsdp", "replica"), None, None),
            P("fsdp"),
            P("fsdp"),
            P("fsdp", None),
            P("fsdp"),
            P("fsdp"),
            P("fsdp", None),
            P("fsdp"),
            P("fsdp"),
            P("fsdp"),
            P("fsdp", None),
            P("fsdp"),
            P("fsdp", None),
            P("fsdp"),
        ),
        check_vma=False,
    )
```

profile of v0, /device:TPU:1, one launch (start us, length us, event | category | flops | bytes accessed | tf_op | source)
XLA Modules:
  0.0 7154.1 jit_solution(2888771679025506342)
XLA Ops:
  8.7 10.3 all-gather.3
  19.7 9.3 all-gather.2
  29.7 36.0 all-gather.5
  66.3 33.2 all-gather.4
  100.8 336.6 %all-gather.17.cloned.1.call-done = bf16[2048,6144]{1,0:T(8,128)(2,1)} async-done(((bf16[512,6144]{1,0:T(8,128)(2,1)}), bf16[2048,6144]{1,0:T(8,128)(2,1)}) %all-gather.17.cloned.1.call-update) | async-done | bytes 25165840 | tf_op jit(solution)/shard_map/all_gather | solution.py:79
  437.4 11.9 fusion.87
  458.9 9.7 all-gather.6
  469.3 10.2 all_gather.61
  479.6 9.7 all-gather.8
  489.3 9.3 all-gather.7
  503.1 7.4 fusion.7
  510.6 6.0 pad_maximum_fusion
  516.6 6.7 copy.54
  526.8 6.0 pad_maximum_fusion.1
  532.8 6.9 copy.56
  540.9 48.0 while.26
  589.0 88.8 %all-gather.19.cloned.1.call-done = bf16[2048,2048]{1,0:T(8,128)(2,1)} async-done(((bf16[512,2048]{1,0:T(8,128)(2,1)}), bf16[2048,2048]{1,0:T(8,128)(2,1)}) %all-gather.19.cloned.1.call-update) | async-done | bytes 8388624 | tf_op jit(solution)/shard_map/all_gather | solution.py:82
  677.7 6.6 fusion.82
  686.1 552.7 %all-gather.21.cloned.1.call-done = bf16[2048,8192]{1,0:T(8,128)(2,1)} async-done(((bf16[512,8192]{1,0:T(8,128)(2,1)}), bf16[2048,8192]{1,0:T(8,128)(2,1)}) %all-gather.21.cloned.1.call-update) | async-done | bytes 33554448 | tf_op jit(solution)/shard_map/all_gather | solution.py:86
  1238.8 34.7 multiply_convert_fusion.1
  1273.5 526.4 %all-gather.23.cloned.1.call-done = bf16[8192,2048]{1,0:T(8,128)(2,1)} async-done(((bf16[2048,2048]{1,0:T(8,128)(2,1)}), bf16[8192,2048]{1,0:T(8,128)(2,1)}) %all-gather.23.cloned.1.call-update) | async-done | bytes 33554448 | tf_op jit(solution)/shard_map/all_gather | solution.py:88
  1799.8 36.5 fusion.83
  1836.4 17.0 multiply_reduce_fusion.1
  1854.9 6.8 convolution_convert_fusion.3
  1862.0 6.9 fusion.32
  1870.2 188.6 %while.27 = (s32[]{:T(128)}, bf16[4,1,272,512]{2,3,1,0:T(8,128)(2,1)}, f32[4,1,1138,512]{2,3,1,0:T(8,128)}, f32[4,1,1138,512]{2,3,1,0:T(8,128)}, s32[4]{0:T(128)...) while((s32[]{:T(128)}, ...), condition=%wide.region_14.15_spmd, body=%wide.region_12.14_spmd.sunk | while | flops 1604632448 | bytes 115616344 | solution.py:240
  1875.5 5.4 fusion.150
  1884.6 8.4 multiply_reduce_fusion.8
  1893.0 10.1 multiply_convert_fusion.3
  1903.1 4.2 fusion.151
  1908.1 5.6 fusion.152
  1922.6 5.4 fusion.150
  1931.8 8.3 multiply_reduce_fusion.8
  1940.1 10.1 multiply_convert_fusion.3
  1950.2 4.2 fusion.151
  1955.2 5.5 fusion.152
  1969.7 5.4 fusion.150
  1978.8 8.4 multiply_reduce_fusion.8
  1987.2 10.1 multiply_convert_fusion.3
  1997.3 4.3 fusion.151
  2002.4 5.6 fusion.152
  2016.9 5.4 fusion.150
  2026.1 8.3 multiply_reduce_fusion.8
  2034.4 10.0 multiply_convert_fusion.3
  2049.4 5.5 fusion.152
  2060.4 10.1 slice.62
  2070.5 6.2 slice.61
  2077.8 21.4 copy.74
  2099.3 21.4 copy.73
  2120.7 2492.1 %all-reduce.20 = (bf16[1,50,2048]{2,0,1:T(2,128)(2,1)S(1)}, bf16[1,50,2048]{2,0,1:T(2,128)(2,1)S(1)}, bf16[1,1088,2048]{2,0,1:T(2,128)(2,1)}, bf16[1,1088,2048]{2,0,1:T(2,128)(2,1)}) all-reduce(f32[1,50,2048]{2,0,1:T(1,128)S(1)} %copy.76, f32[1,50,2048]{2,0,1:T(1,128)S(1)} %copy.75, ...), channel_id=1, replica_groups=mesh['fsdp'=4,'replica'=2,'ctx'=4] {'ctx'}, use_global_device_ids=true, to_apply=%region_20.21 | all-reduce | flops 4661248 | bytes 27967488 | tf_op jit(solution)/shard_map/psum | solution.py:248
  4617.4 4.3 constant_dynamic-slice_fusion.8
  4629.4 17.2 convolution_convert_fusion.2
  4648.3 24.3 convolution_convert_fusion.1
  4673.8 24.3 convolution_convert_fusion
  4698.8 11.8 all-gather.9
  4712.8 12.2 fusion.69
  4731.5 14.9 fusion.40
  4746.5 19.0 all-reduce.17
  4766.1 4.5 fusion.39
  4770.6 17.5 fusion.31
  4788.1 272.3 %reduce-scatter.9.cloned.1.call-done = bf16[512,6144]{1,0:T(8,128)(2,1)} async-done(((bf16[2048,6144]{1,0:T(8,128)(2,1)}), bf16[512,6144]{1,0:T(8,128)(2,1)}) %reduce-scatter.9.cloned.1.call-update) | async-done | bytes 6291472 | tf_op jit(solution)/shard_map/reduce_scatter | solution.py:298
  5060.4 556.3 %reduce-scatter.13.cloned.1.call-done = bf16[512,8192]{1,0:T(8,128)(2,1)} async-done(((bf16[2048,8192]{1,0:T(8,128)(2,1)}), bf16[512,8192]{1,0:T(8,128)(2,1)}) %reduce-scatter.13.cloned.1.call-update) | async-done | bytes 8388624
  5616.7 555.0 %reduce-scatter.15.cloned.1.call-done = bf16[2048,2048]{1,0:T(8,128)(2,1)} async-done(((bf16[8192,2048]{1,0:T(8,128)(2,1)}), bf16[2048,2048]{1,0:T(8,128)(2,1)}) %reduce-scatter.15.cloned.1.call-update) | async-done | bytes 8388624
  6171.8 975.3 %all-reduce.21 = (f32[512]{0:T(512)}, f32[512]{0:T(512)}, f32[512,6144]{1,0:T(8,128)}, f32[512]{0:T(512)}, f32[512]{0:T(512)}, /*index=5*/f32[512,2048]{1,0:T(8,...) all-reduce(f32[512]{0:T(512)S(1)} %dynamic-slice_convert_fusion.8, ...), channel_id=1, replica_groups=mesh['fsdp'=4,'replica'=2,'ctx'=4] {'replica','ctx'}, use_global_device_ids=true, to_apply=%region_26.27 | all-reduce | flops 12589056 | bytes 75546624 | tf_op jit(solution)/shard_map/psum | solution.py:326
  (316 shorter events, 146.1 us)
Async XLA Ops:
  7.2 92.4 %copy-start.2 = (bf16[1,272,2048]{2,1,0:T(8,128)(2,1)S(1)}, bf16[1,272,2048]{2,1,0:T(8,128)(2,1)}, u32[]{:S(2)}) copy-start(bf16[1,272,2048]{2,1,0:T(8,128)(2,1)} %param.21) | copy-start | bytes 3342340
  7.2 430.2 %all-gather.17.cloned.1.call-start = ((), (), s32[]{:S(2)}) async-start(), calls=%async_computation.4 | async-start | bytes 31457280 | tf_op jit(solution)/shard_map/all_gather | solution.py:79
  7.9 502.7 %all-gather.25.cloned.1.call-start = ((), (), s32[]{:S(2)}) async-start(), calls=%async_computation.10 | async-start | bytes 5570560 | tf_op jit(solution)/shard_map/all_gather | solution.py:131
  29.0 472.0 %copy-start.25 = (f32[4,1,512]{2,1,0:T(1,128)}, f32[4,1,512]{2,1,0:T(1,128)S(1)}, u32[]{:S(2)}) copy-start(f32[4,1,512]{2,1,0:T(1,128)S(1)} %convert_element_type.263) | copy-start | bytes 24580
  99.8 349.5 %copy-start.29 = (f32[272]{0:T(512)}, f32[272]{0:T(512)S(1)}, u32[]{:S(2)}) copy-start(f32[272]{0:T(512)S(1)} %broadcast_multiply_fusion.5) | copy-start | bytes 3268
  100.3 349.1 %copy-start.33 = (f32[272]{0:T(512)}, f32[272]{0:T(512)S(1)}, u32[]{:S(2)}) copy-start(f32[272]{0:T(512)S(1)} %add_rsqrt_fusion.1) | copy-start | bytes 3268
  100.8 348.6 %copy-start.18 = (bf16[272,2048]{1,0:T(8,128)(2,1)}, bf16[272,2048]{1,0:T(8,128)(2,1)S(1)}, u32[]{:S(2)}) copy-start(bf16[272,2048]{1,0:T(8,128)(2,1)S(1)} %fusion.34) | copy-start | bytes 3342340
  449.4 2.8 copy-start.12
  454.2 72.7 %all-gather.27.cloned.1.call-start = ((), (), s32[]{:S(2)}) async-start(), calls=%async_computation.11 | async-start | bytes 5570560 | tf_op jit(solution)/shard_map/all_gather | solution.py:130
  457.0 220.7 %all-gather.19.cloned.1.call-start = ((), (), s32[]{:S(2)}) async-start(), calls=%async_computation.5 | async-start | bytes 10485760 | tf_op jit(solution)/shard_map/all_gather | solution.py:82
  457.6 11.7 copy-start.43
  457.6 21.9 copy-start.49
  457.6 31.6 copy-start.50
  457.6 41.0 copy-start.53
  457.7 42.2 copy-start.17
  457.7 781.1 %all-gather.21.cloned.1.call-start = ((), (), s32[]{:S(2)}) async-start(), calls=%async_computation.6 | async-start | bytes 41943040 | tf_op jit(solution)/shard_map/all_gather | solution.py:86
  458.3 1341.6 %all-gather.23.cloned.1.call-start = ((), (), s32[]{:S(2)}) async-start(), calls=%async_computation.7 | async-start | bytes 41943040 | tf_op jit(solution)/shard_map/all_gather | solution.py:88
  458.8 4329.3 %reduce-scatter.11.cloned.1.call-start = ((), (), s32[]{:S(2)}) async-start(), calls=%async_computation.9 | async-start | bytes 10485760 | tf_op jit(solution)/shard_map/reduce_scatter | solution.py:307
  489.3 749.5 %copy-start.39 = (f32[4,1,512]{2,1,0:T(1,128)}, f32[4,1,512]{2,1,0:T(1,128)S(1)}, u32[]{:S(2)}) copy-start(f32[4,1,512]{2,1,0:T(1,128)S(1)} %convert_element_type.269) | copy-start | bytes 24580
  498.6 1354.8 %copy-start.27 = (f32[4,1,512]{2,1,0:T(1,128)}, f32[4,1,512]{2,1,0:T(1,128)S(1)}, u32[]{:S(2)}) copy-start(f32[4,1,512]{2,1,0:T(1,128)S(1)} %convert_element_type.268) | copy-start | bytes 24580
  500.0 10.5 copy-start.41
  500.3 10.2 copy-start.46
  501.1 1.9 copy-start.23
  589.0 95.4 %copy-start = (pred[1,1,272,1138]{3,2,1,0:T(8,128)(4,1)}, pred[1,1,272,1138]{3,2,1,0:T(8,128)(4,1)S(1)}, u32[]{:S(2)}) copy-start(pred[1,1,272,1138]{3,2,1,0:T(8,128)(4,1)S(1)} %get-tuple-element.553) | copy-start | bytes 928612
  589.0 95.4 %copy-start.7 = (bf16[1,272,2048]{1,2,0:T(8,128)(2,1)}, bf16[1,272,2048]{1,2,0:T(8,128)(2,1)S(1)}, u32[]{:S(2)}) copy-start(bf16[1,272,2048]{1,2,0:T(8,128)(2,1)S(1)} %get-tuple-element.562) | copy-start | bytes 3342340
  684.4 1169.1 %copy-start.31 = (f32[272]{0:T(512)}, f32[272]{0:T(512)S(1)}, u32[]{:S(2)}) copy-start(f32[272]{0:T(512)S(1)} %broadcast_multiply_fusion.4) | copy-start | bytes 3268
  686.1 1167.3 %copy-start.37 = (f32[272]{0:T(512)}, f32[272]{0:T(512)S(1)}, u32[]{:S(2)}) copy-start(f32[272]{0:T(512)S(1)} %add_rsqrt_fusion) | copy-start | bytes 3268
  1238.8 561.0 %copy-start.13 = (bf16[1,272,2048]{2,1,0:T(8,128)(2,1)S(1)}, bf16[1,272,2048]{2,1,0:T(8,128)(2,1)}, u32[]{:S(2)}) copy-start(bf16[1,272,2048]{2,1,0:T(8,128)(2,1)} %param.24) | copy-start | bytes 3342340
  1799.8 36.5 copy-start.5
  1836.4 17.1 copy-start.14
  1854.9 7.1 copy-start.9
  1861.8 8.4 copy-start.1
  1861.8 3198.6 %reduce-scatter.9.cloned.1.call-start = ((), (), s32[]{:S(2)}) async-start(), calls=%async_computation.8 | async-start | bytes 31457280 | tf_op jit(solution)/shard_map/reduce_scatter | solution.py:298
  1907.3 6.4 slice-start
  1908.1 5.6 slice-start.1
  1954.4 6.4 slice-start
  1955.2 5.6 slice-start.1
  2001.6 6.5 slice-start
  2002.4 5.7 slice-start.1
  2048.6 6.4 slice-start
  2049.4 5.6 slice-start.1
  2058.9 11.6 slice-start.2
  2060.3 10.1 slice-start.3
  2060.3 10.1 slice-start.4
  4616.7 6.6 copy-start.11
  4617.4 8.2 copy-start.16
  4625.2 4.3 copy-start.19
  4625.2 4.2 copy-start.24
  4625.3 2.3 copy-start.21
  4625.5 2.2 copy-start.22
  4625.6 2.1 copy-start.20
  4646.7 970.0 %reduce-scatter.13.cloned.1.call-start = ((), (), s32[]{:S(2)}) async-start(), calls=%async_computation.12 | async-start | bytes 41943040
  4672.6 1499.1 %reduce-scatter.15.cloned.1.call-start = ((), (), s32[]{:S(2)}) async-start(), calls=%async_computation.13 | async-start | bytes 41943040
  4698.1 12.7 copy-start.52
  4698.1 14.6 copy-start.26
  4698.1 14.6 copy-start.42
  4698.2 14.6 copy-start.47
  4712.8 18.7 copy-start.3
  4712.8 18.7 copy-start.30
  4712.8 18.7 copy-start.34
  4731.5 15.0 copy-start.35
  4731.5 15.0 copy-start.36
  4731.5 15.0 copy-start.44
  4731.5 15.0 copy-start.45
  (11 other events, 16.0 us)
Sparse Core Ops, SparseCore 0:
  9.6 427.7 all-gather.16
  454.3 34.3 all-gather.24
  490.8 35.9 all-gather.26
  528.2 149.4 all-gather.18
  679.1 559.6 all-gather.20
  1240.2 559.5 all-gather.22
  1861.9 142.2 reduce-scatter.10
  4646.8 413.5 reduce-scatter.8
  5062.9 553.7 reduce-scatter.12
  5619.0 552.7 reduce-scatter.14
where the time goes:
time: 7170 us; the launch traced here: 7150 us
  blocking collectives  3630 us (51%)
  waiting for transfers between devices  2890 us (40%)
  matrix products  356 us (5%)
  local copies, waits for them, and re-layouts  161 us (2%)
  other arithmetic  84.4 us (1%)
    psum x1, blocking collectives, shards(): lax.psum((key_grad_all[:, :SUMM], value_grad_all[:, :SUMM]), 'ctx')  2490 us
    unnamed x12, waiting for transfers between devices  1110 us
    psum x1, blocking collectives, shards(): lax.psum((shares[0], shares[1], shares[2], shares[3], shares[4], shares[5...  975 us
    all_gather x1, waiting for transfers between devices, shards(): lax.all_gather(up_weight, 'fsdp', axis=0, tiled=True)  553 us
    all_gather x1, waiting for transfers between devices, shards(): lax.all_gather(down_weight, 'fsdp', axis=0, tiled=True)  526 us
    all_gather x1, waiting for transfers between devices, shards(): lax.all_gather(qkv_weight, 'fsdp', axis=0, tiled=True)  337 us
    reduce_scatter x1, waiting for transfers between devices, shards(): lax.psum_scatter(qkv_weight_grad.astype(jnp.bfloat16), 'fsdp', scatter_di...  272 us
  transfers between devices with their start and end apart: 10, of which 8 were waited for; matrix products, arithmetic and copies ran while one was open for 7% of the time, Pallas kernels for 0%

commit v1 on v0

--- a/solution.py
+++ b/solution.py
@@ -323,24 +323,23 @@
             down_bias_grad.astype(jnp.bfloat16), "fsdp", scatter_dimension=0, tiled=True
         ).astype(jnp.float32),
     )
-    summed = lax.psum(
-        (
-            shares[0],
-            shares[1],
-            shares[2],
-            shares[3],
-            shares[4],
-            shares[5],
-            shares[6],
-            shares[7],
-            shares[8],
-            shares[9],
-            shares[10],
-            up_part,
-            down_part,
-        ),
-        ("replica", "ctx"),
-    )
+    summed = (
+        shares[0],
+        shares[1],
+        shares[2],
+        shares[3],
+        shares[4],
+        shares[5],
+        shares[6],
+        shares[7],
+        shares[8],
+        shares[9],
+        shares[10],
+        up_part,
+        down_part,
+    )
+    for over in ("ctx", "replica"):
+        summed = lax.psum(summed, over)
     return (
         output,
         input_grad,

time: 7170 us -> 8180 us (1.14)
  waiting for transfers between devices: 2890 us -> 3990 us
  blocking collectives: 3630 us -> 3500 us
    psum x0 -> x1, waiting for transfers between devices: none -> 1060 us  [shards(): summed = lax.psum(summed, over)]
    psum x1 -> x2, blocking collectives: 975 us -> 856 us  [shards(): summed = lax.psum(summed, over)]
    unnamed x12 -> x13, waiting for transfers between devices: 1110 us -> 1110 us
  transfers between devices with their start and end apart: 10 -> 11, of which waited for: 8 -> 9; matrix products, arithmetic and copies ran while one was open for 7% -> 6% of each run, Pallas kernels for 0% -> 0%
where the time goes in v1:
time: 8180 us; the launch traced here: 8170 us
  waiting for transfers between devices  3990 us (49%)
  blocking collectives  3500 us (43%)
  matrix products  356 us (4%)
  local copies, waits for them, and re-layouts  197 us (2%)
  other arithmetic  84.4 us (1%)
    psum x1, blocking collectives, shards(): lax.psum((key_grad_all[:, :SUMM], value_grad_all[:, :SUMM]), 'ctx')  2490 us
    unnamed x13, waiting for transfers between devices  1110 us
    psum x1, waiting for transfers between devices, shards(): summed = lax.psum(summed, over)  1060 us
    psum x2, blocking collectives, shards(): summed = lax.psum(summed, over)  856 us
    all_gather x1, waiting for transfers between devices, shards(): lax.all_gather(up_weight, 'fsdp', axis=0, tiled=True)  553 us
    all_gather x1, waiting for transfers between devices, shards(): lax.all_gather(down_weight, 'fsdp', axis=0, tiled=True)  526 us
    all_gather x1, waiting for transfers between devices, shards(): lax.all_gather(qkv_weight, 'fsdp', axis=0, tiled=True)  337 us
    reduce_scatter x1, waiting for transfers between devices, shards(): lax.psum_scatter(qkv_weight_grad.astype(jnp.bfloat16), 'fsdp', scatter_di...  310 us
  transfers between devices with their start and end apart: 11, of which 9 were waited for; matrix products, arithmetic and copies ran while one was open for 6% of the time, Pallas kernels for 0%

profile of v1, /device:TPU:1, one launch (start us, length us, event | category | flops | bytes accessed | tf_op | source)
XLA Modules:
  0.0 8166.6 jit_solution(13841071836612689876)
XLA Ops:
  8.7 10.3 all-gather.3
  19.7 9.3 all-gather.2
  29.7 36.0 all-gather.5
  66.3 33.2 all-gather.4
  100.8 336.6 %all-gather.17.cloned.1.call-done = bf16[2048,6144]{1,0:T(8,128)(2,1)} async-done(((bf16[512,6144]{1,0:T(8,128)(2,1)}), bf16[2048,6144]{1,0:T(8,128)(2,1)}) %all-gather.17.cloned.1.call-update) | async-done | bytes 25165840 | tf_op jit(solution)/shard_map/all_gather | solution.py:79
  437.4 11.9 fusion.87
  458.9 9.7 all-gather.6
  469.3 10.2 all_gather.61
  479.5 9.7 all-gather.8
  489.2 9.3 all-gather.7
  503.0 7.4 fusion.7
  510.6 6.0 pad_maximum_fusion
  516.6 6.7 copy.54
  526.8 6.0 pad_maximum_fusion.1
  532.7 6.8 copy.56
  540.9 48.1 while.26
  588.9 88.7 %all-gather.19.cloned.1.call-done = bf16[2048,2048]{1,0:T(8,128)(2,1)} async-done(((bf16[512,2048]{1,0:T(8,128)(2,1)}), bf16[2048,2048]{1,0:T(8,128)(2,1)}) %all-gather.19.cloned.1.call-update) | async-done | bytes 8388624 | tf_op jit(solution)/shard_map/all_gather | solution.py:82
  677.7 6.6 fusion.82
  686.1 552.7 %all-gather.21.cloned.1.call-done = bf16[2048,8192]{1,0:T(8,128)(2,1)} async-done(((bf16[512,8192]{1,0:T(8,128)(2,1)}), bf16[2048,8192]{1,0:T(8,128)(2,1)}) %all-gather.21.cloned.1.call-update) | async-done | bytes 33554448 | tf_op jit(solution)/shard_map/all_gather | solution.py:86
  1238.8 34.7 multiply_convert_fusion.1
  1273.4 526.4 %all-gather.23.cloned.1.call-done = bf16[8192,2048]{1,0:T(8,128)(2,1)} async-done(((bf16[2048,2048]{1,0:T(8,128)(2,1)}), bf16[8192,2048]{1,0:T(8,128)(2,1)}) %all-gather.23.cloned.1.call-update) | async-done | bytes 33554448 | tf_op jit(solution)/shard_map/all_gather | solution.py:88
  1799.8 36.4 fusion.83
  1836.2 17.0 multiply_reduce_fusion.1
  1854.8 6.8 convolution_convert_fusion.3
  1861.8 6.9 fusion.32
  1870.1 188.6 %while.27 = (s32[]{:T(128)}, bf16[4,1,272,512]{2,3,1,0:T(8,128)(2,1)}, f32[4,1,1138,512]{2,3,1,0:T(8,128)}, f32[4,1,1138,512]{2,3,1,0:T(8,128)}, s32[4]{0:T(128)...) while((s32[]{:T(128)}, ...), condition=%wide.region_14.15_spmd, body=%wide.region_12.14_spmd.sunk | while | flops 1604632448 | bytes 115616344 | solution.py:240
  1875.3 5.4 fusion.150
  1884.4 8.4 multiply_reduce_fusion.8
  1892.8 10.1 multiply_convert_fusion.3
  1907.9 5.6 fusion.152
  1922.4 5.4 fusion.150
  1931.6 8.3 multiply_reduce_fusion.8
  1939.9 10.1 multiply_convert_fusion.3
  1955.0 5.5 fusion.152
  1969.5 5.4 fusion.150
  1978.6 8.4 multiply_reduce_fusion.8
  1987.0 10.1 multiply_convert_fusion.3
  2002.2 5.6 fusion.152
  2016.7 5.4 fusion.150
  2025.9 8.3 multiply_reduce_fusion.8
  2034.2 10.0 multiply_convert_fusion.3
  2049.2 5.5 fusion.152
  2060.1 10.1 slice.62
  2070.3 6.2 slice.61
  2077.6 21.4 copy.74
  2099.0 21.4 copy.73
  2120.5 2492.1 %all-reduce.25 = (bf16[1,50,2048]{2,0,1:T(2,128)(2,1)S(1)}, bf16[1,50,2048]{2,0,1:T(2,128)(2,1)S(1)}, bf16[1,1088,2048]{2,0,1:T(2,128)(2,1)}, bf16[1,1088,2048]{2,0,1:T(2,128)(2,1)}) all-reduce(f32[1,50,2048]{2,0,1:T(1,128)S(1)} %copy.76, f32[1,50,2048]{2,0,1:T(1,128)S(1)} %copy.75, ...), channel_id=1, replica_groups=mesh['fsdp'=4,'replica'=2,'ctx'=4] {'ctx'}, use_global_device_ids=true, to_apply=%region_20.21 | all-reduce | flops 4661248 | bytes 27967488 | tf_op jit(solution)/shard_map/psum | solution.py:248
  4629.2 17.1 convolution_convert_fusion.2
  4648.0 24.3 convolution_convert_fusion.1
  4673.5 24.3 convolution_convert_fusion
  4704.3 12.2 fusion.69
  4716.6 14.9 fusion.40
  4731.5 17.9 all-reduce.19
  4750.0 310.0 %reduce-scatter.9.cloned.1.call-done = bf16[512,6144]{1,0:T(8,128)(2,1)} async-done(((bf16[2048,6144]{1,0:T(8,128)(2,1)}), bf16[512,6144]{1,0:T(8,128)(2,1)}) %reduce-scatter.9.cloned.1.call-update) | async-done | bytes 6291472 | tf_op jit(solution)/shard_map/reduce_scatter | solution.py:298
  5060.1 556.3 %reduce-scatter.13.cloned.1.call-done = bf16[512,8192]{1,0:T(8,128)(2,1)} async-done(((bf16[2048,8192]{1,0:T(8,128)(2,1)}), bf16[512,8192]{1,0:T(8,128)(2,1)}) %reduce-scatter.13.cloned.1.call-update) | async-done | bytes 8388624
  5616.3 555.0 %reduce-scatter.15.cloned.1.call-done = bf16[2048,2048]{1,0:T(8,128)(2,1)} async-done(((bf16[8192,2048]{1,0:T(8,128)(2,1)}), bf16[2048,2048]{1,0:T(8,128)(2,1)}) %reduce-scatter.15.cloned.1.call-update) | async-done | bytes 8388624
  6171.4 848.1 %all-reduce.26 = (f32[512]{0:T(512)S(1)}, f32[512]{0:T(512)S(1)}, f32[512,6144]{1,0:T(8,128)}, f32[512]{0:T(512)S(1)}, f32[512]{0:T(512)S(1)}, /*index=5*/f32[51...) all-reduce(f32[512]{0:T(512)S(1)} %dynamic-slice_convert_fusion.8, ...), channel_id=1, replica_groups=mesh['fsdp'=4,'replica'=2,'ctx'=4] {'ctx'}, use_global_device_ids=true, to_apply=%region_26.27 | all-reduce | flops 12589056 | bytes 75546624 | tf_op jit(solution)/shard_map/psum | solution.py:342
  7020.1 10.2 all-gather.9
  7037.4 17.2 fusion.31
  7054.6 8.4 all-reduce.17
  7063.0 1061.6 %all-reduce.24.cloned.1.call-done = (f32[512,6144]{1,0:T(8,128)}, f32[512,2048]{1,0:T(8,128)}, f32[512,8192]{1,0:T(8,128)}, f32[2048,2048]{1,0:T(8,128)}) async-done(((f32[512,6144]{1,0:T(8,128)}, f32[512,2048]{1,0:T(8,128)}, f32[512,8192]{1,0:T(8,128)}, f32[2048,2048]{1,0:T(8,128)}), (f32[512,6144]{1,0:T(8,128)}, f32[512,2048]{1,0:T(8,128)}, f32[512,8192]{1,0:T(8,128)}, ...) | async-done | bytes 50331664 | tf_op jit(solution)/shard_map/psum | solution.py:342
  8124.6 11.0 copy.140
  8137.7 13.9 copy.142
  8153.8 6.2 copy.143
  (340 shorter events, 172.4 us)
Async XLA Ops:
  7.2 92.4 %copy-start.2 = (bf16[1,272,2048]{2,1,0:T(8,128)(2,1)S(1)}, bf16[1,272,2048]{2,1,0:T(8,128)(2,1)}, u32[]{:S(2)}) copy-start(bf16[1,272,2048]{2,1,0:T(8,128)(2,1)} %param.21) | copy-start | bytes 3342340
  7.2 430.2 %all-gather.17.cloned.1.call-start = ((), (), s32[]{:S(2)}) async-start(), calls=%async_computation.4 | async-start | bytes 31457280 | tf_op jit(solution)/shard_map/all_gather | solution.py:79
  7.9 502.7 %all-gather.25.cloned.1.call-start = ((), (), s32[]{:S(2)}) async-start(), calls=%async_computation.10 | async-start | bytes 5570560 | tf_op jit(solution)/shard_map/all_gather | solution.py:131
  29.0 472.0 %copy-start.26 = (f32[4,1,512]{2,1,0:T(1,128)}, f32[4,1,512]{2,1,0:T(1,128)S(1)}, u32[]{:S(2)}) copy-start(f32[4,1,512]{2,1,0:T(1,128)S(1)} %convert_element_type.263) | copy-start | bytes 24580
  99.8 349.5 %copy-start.30 = (f32[272]{0:T(512)}, f32[272]{0:T(512)S(1)}, u32[]{:S(2)}) copy-start(f32[272]{0:T(512)S(1)} %broadcast_multiply_fusion.5) | copy-start | bytes 3268
  100.3 349.0 %copy-start.34 = (f32[272]{0:T(512)}, f32[272]{0:T(512)S(1)}, u32[]{:S(2)}) copy-start(f32[272]{0:T(512)S(1)} %add_rsqrt_fusion.1) | copy-start | bytes 3268
  100.8 348.5 %copy-start.19 = (bf16[272,2048]{1,0:T(8,128)(2,1)}, bf16[272,2048]{1,0:T(8,128)(2,1)S(1)}, u32[]{:S(2)}) copy-start(bf16[272,2048]{1,0:T(8,128)(2,1)S(1)} %fusion.34) | copy-start | bytes 3342340
  454.1 72.7 all-gather.27.cloned.1.call-start
  457.0 220.7 %all-gather.19.cloned.1.call-start = ((), (), s32[]{:S(2)}) async-start(), calls=%async_computation.5 | async-start | bytes 10485760 | tf_op jit(solution)/shard_map/all_gather | solution.py:82
  457.6 11.7 copy-start.44
  457.6 21.9 copy-start.50
  457.6 31.6 copy-start.51
  457.6 41.0 copy-start.54
  457.6 42.2 copy-start.18
  457.6 781.1 %all-gather.21.cloned.1.call-start = ((), (), s32[]{:S(2)}) async-start(), calls=%async_computation.6 | async-start | bytes 41943040 | tf_op jit(solution)/shard_map/all_gather | solution.py:86
  458.2 1341.6 %all-gather.23.cloned.1.call-start = ((), (), s32[]{:S(2)}) async-start(), calls=%async_computation.7 | async-start | bytes 41943040 | tf_op jit(solution)/shard_map/all_gather | solution.py:88
  458.8 4291.2 %reduce-scatter.11.cloned.1.call-start = ((), (), s32[]{:S(2)}) async-start(), calls=%async_computation.9 | async-start | bytes 10485760 | tf_op jit(solution)/shard_map/reduce_scatter | solution.py:307
  489.2 749.5 %copy-start.40 = (f32[4,1,512]{2,1,0:T(1,128)}, f32[4,1,512]{2,1,0:T(1,128)S(1)}, u32[]{:S(2)}) copy-start(f32[4,1,512]{2,1,0:T(1,128)S(1)} %convert_element_type.269) | copy-start | bytes 24580
  498.5 1354.8 %copy-start.28 = (f32[4,1,512]{2,1,0:T(1,128)}, f32[4,1,512]{2,1,0:T(1,128)S(1)}, u32[]{:S(2)}) copy-start(f32[4,1,512]{2,1,0:T(1,128)S(1)} %convert_element_type.268) | copy-start | bytes 24580
  500.0 10.5 copy-start.42
  500.2 10.2 copy-start.47
  588.9 95.4 %copy-start = (pred[1,1,272,1138]{3,2,1,0:T(8,128)(4,1)}, pred[1,1,272,1138]{3,2,1,0:T(8,128)(4,1)S(1)}, u32[]{:S(2)}) copy-start(pred[1,1,272,1138]{3,2,1,0:T(8,128)(4,1)S(1)} %get-tuple-element.590) | copy-start | bytes 928612
  588.9 95.4 %copy-start.7 = (bf16[1,272,2048]{1,2,0:T(8,128)(2,1)}, bf16[1,272,2048]{1,2,0:T(8,128)(2,1)S(1)}, u32[]{:S(2)}) copy-start(bf16[1,272,2048]{1,2,0:T(8,128)(2,1)S(1)} %get-tuple-element.599) | copy-start | bytes 3342340
  684.3 1169.0 %copy-start.32 = (f32[272]{0:T(512)}, f32[272]{0:T(512)S(1)}, u32[]{:S(2)}) copy-start(f32[272]{0:T(512)S(1)} %broadcast_multiply_fusion.4) | copy-start | bytes 3268
  686.1 1167.2 %copy-start.38 = (f32[272]{0:T(512)}, f32[272]{0:T(512)S(1)}, u32[]{:S(2)}) copy-start(f32[272]{0:T(512)S(1)} %add_rsqrt_fusion) | copy-start | bytes 3268
  1238.8 561.0 %copy-start.13 = (bf16[1,272,2048]{2,1,0:T(8,128)(2,1)S(1)}, bf16[1,272,2048]{2,1,0:T(8,128)(2,1)}, u32[]{:S(2)}) copy-start(bf16[1,272,2048]{2,1,0:T(8,128)(2,1)} %param.24) | copy-start | bytes 3342340
  1799.8 36.4 copy-start.5
  1836.2 17.1 copy-start.14
  1854.8 7.0 copy-start.9
  1861.6 8.4 copy-start.1
  1861.6 3198.4 %reduce-scatter.9.cloned.1.call-start = ((), (), s32[]{:S(2)}) async-start(), calls=%async_computation.8 | async-start | bytes 31457280 | tf_op jit(solution)/shard_map/reduce_scatter | solution.py:298
  1907.1 6.4 slice-start
  1907.9 5.6 slice-start.1
  1954.2 6.4 slice-start
  1955.0 5.6 slice-start.1
  2001.4 6.5 slice-start
  2002.2 5.7 slice-start.1
  2048.4 6.4 slice-start
  2049.2 5.6 slice-start.1
  2058.7 11.6 slice-start.6
  2060.1 10.1 slice-start.7
  2060.1 10.1 slice-start.8
  4616.5 6.6 copy-start.11
  4617.1 8.2 copy-start.16
  4646.4 970.0 %reduce-scatter.13.cloned.1.call-start = ((), (), s32[]{:S(2)}) async-start(), calls=%async_computation.12 | async-start | bytes 41943040
  4672.3 1499.1 %reduce-scatter.15.cloned.1.call-start = ((), (), s32[]{:S(2)}) async-start(), calls=%async_computation.13 | async-start | bytes 41943040
  4697.8 6.4 copy-start.27
  4697.8 6.5 copy-start.43
  4697.8 6.5 copy-start.48
  4697.8 3426.8 %all-reduce.24.cloned.1.call-start = ((), (), s32[]{:S(2)}) async-start(), calls=%async_computation.14 | async-start | bytes 100663296 | tf_op jit(solution)/shard_map/psum | solution.py:342
  4704.3 12.2 copy-start.3
  4704.3 12.2 copy-start.31
  4704.3 12.2 copy-start.35
  4716.5 14.9 copy-start.36
  4716.5 14.9 copy-start.37
  4716.5 14.9 copy-start.45
  4716.6 14.9 copy-start.46
  7020.1 17.3 slice-start.9
  7032.9 4.5 slice-start.10
  8124.6 11.0 copy-start.17
  8135.6 16.0 slice-start.2
  8137.7 13.9 slice-start.3
  8137.7 14.4 slice-start.4
  8137.7 16.0 slice-start.5
  (19 other events, 36.6 us)
Sparse Core Ops, SparseCore 0:
  9.6 427.7 all-gather.16
  454.2 34.3 all-gather.24
  490.8 35.9 all-gather.26
  528.2 149.4 all-gather.18
  679.1 559.6 all-gather.20
  1240.2 559.5 all-gather.22
  1861.7 142.2 reduce-scatter.10
  4646.5 413.5 reduce-scatter.8
  5062.5 553.7 reduce-scatter.12
  5618.5 552.7 reduce-scatter.14
  7019.6 1104.9 all-reduce.23
